TPU v7x, 768 devices: a whole 4x8x12 slice. The times are simulated.
768 devices in a mesh: grp: 192 (over y, z, core), dev: 4 (over x).
Axes of the slice: x: 4, y: 8, z: 12, core: 2. Of those that a mesh axis runs over, the one named last changes fastest.
Arguments:
- operators: bfloat16 [1536, 1024, 1024], P(('grp', 'dev')), may hold values from -0.3 to 2.3, as said below
- forces: float32 [1536, 32, 512], P(('grp', 'dev')), may hold values from -48 to 48
- weights: float32 [1536, 512], P(('grp', 'dev')), may hold values from 0.5 to 2
- lengths: int32 [1536], replicated, may hold values from 128 to 512, as said below
- slot_order: int32 [1536, 512], P(('grp', 'dev')), may hold values from 0 to 511, as said below
Outputs:
- solution: float32 [1536, 32, 512], P(('grp', 'dev'))
- residual: float32 [1536, 32, 512], P(('grp', 'dev'))
Inputs may be any that keep to these rules, and one draw needn't show every extreme that they name: `lengths`: every interface has at least 128 live multipliers and some interface has exactly 512; the last entry belongs to the end of the chain and is not used. `slot_order`: row k is a permutation of 0 to 511 that maps the first lengths[k] positions onto the first lengths[k] slots and leaves the other positions in place. `operators`: each operator is symmetric, and positive definite on every subset of its rows and columns.
All inputs are finite; a program needn't handle non-finite values.
Results may differ from a plain program's by a relative error of at most 0.01.
Values may be sent and summed in bfloat16 or wider, within the bound.
No kernel may reach another device: no remote copies, remote signals or barrier semaphores. Data moves between devices by JAX's collectives and lax.ppermute only.
A program may use at most 32 MiB of HBM per device.

v0:
```python
import functools

import jax
import jax.numpy as jnp
from jax import lax
from jax.sharding import Mesh
from jax.sharding import PartitionSpec as P

ITERS = 2
GRP = ("grp_0", "grp_1", "grp_2")
GRP_DEV = ("grp_0", "grp_1", "grp_2", "dev")


def from_everyone(shard, axis):
    peers = lax.axis_size(axis)
    return lax.all_to_all(
        jnp.broadcast_to(shard[None], (peers, *shard.shape)), axis, 0, 0, tiled=True
    )


def taken_together(shard, axis):
    everything = from_everyone(shard, axis)
    return jnp.sum(everything, axis=0)


def over_axes(shard, axes):
    return functools.reduce(lax.psum, axes, shard)


def shifted_2(block, axis, distance):
    devices = range(lax.axis_size(axis))
    route = [(i - distance, i) for i in devices if i - distance in devices]
    return lax.ppermute(block, axis, route)


def cholesky_solve(matrix, target):
    factor = jnp.linalg.cholesky(matrix)
    halfway = lax.linalg.triangular_solve(factor, target, left_side=True, lower=True)
    return lax.linalg.triangular_solve(
        factor, halfway, left_side=True, lower=True, transpose_a=True
    )


def inner(first, second):
    return jnp.einsum("kri,kti->rt", first, second, precision=lax.Precision.HIGHEST)


def combine(field, matrix):
    return jnp.einsum("kri,rt->kti", field, matrix, precision=lax.Precision.HIGHEST)


def totals(stacked):
    within = taken_together(stacked, "dev")
    return over_axes(within, GRP)


def toward_lower(field):
    return shifted_2(field, GRP_DEV, -1)


def column_part(inputs, columns):
    return jnp.dot(inputs, columns, preferred_element_type=jnp.float32)


def body(operators, forces, weights, lengths, slot_order):
    number, load_cases, breadth = forces.shape
    offset = lax.axis_index(GRP_DEV) * number
    chain_total = lengths.shape[0]
    zero_entry = jnp.zeros((1,), jnp.int32)
    padded = jnp.concatenate([zero_entry, lengths, zero_entry])
    window = lax.dynamic_slice_in_dim(padded, offset, number + 2)
    places = offset - 1 + jnp.arange(number + 2, dtype=jnp.int32)
    window = jnp.where((places >= 0) & (places < chain_total - 1), window, 0)
    positions = jnp.arange(breadth, dtype=jnp.int32)
    live_mask = (positions[None, :] < window[1 : number + 1, None]).astype(jnp.float32)[:, None, :]
    inverse = jnp.argsort(slot_order, axis=1)
    residual = live_mask * forces
    solution = jnp.zeros_like(residual)
    search = weights[:, None, :] * residual
    for iteration in range(ITERS):
        turned = jnp.take_along_axis(search, slot_order[:, None, :], axis=2)
        incoming = shifted_2(turned[number - 1].astype(jnp.bfloat16), GRP_DEV, 1).astype(
            jnp.float32
        )
        left_input = jnp.concatenate([incoming[None], turned[:-1]], axis=0)
        inputs = jnp.concatenate([left_input, search], axis=2).astype(jnp.bfloat16)
        rights = [
            column_part(inputs[local], operators[local, :, breadth:]) for local in range(number)
        ]
        owned = [
            column_part(inputs[local], operators[local, :, :breadth]) for local in range(number)
        ]
        returned = toward_lower(owned[0])
        lefts = owned[1:] + [returned]
        shifted = jnp.stack(lefts)
        gathered = jnp.take_along_axis(shifted, inverse[:, None, :], axis=2)
        image = live_mask * (jnp.stack(rights) + gathered)
        if iteration + 1 < ITERS:
            summed = totals(
                jnp.stack(
                    [
                        inner(search, image),
                        inner(search, residual),
                        inner(image, weights[:, None, :] * residual),
                        inner(image, weights[:, None, :] * image),
                    ]
                )
            )
        else:
            summed = totals(jnp.stack([inner(search, image), inner(search, residual)]))
        curvature = summed[0]
        alpha = cholesky_solve(curvature, summed[1])
        solution = solution + combine(search, alpha)
        residual = residual - combine(image, alpha)
        if iteration + 1 < ITERS:
            scaled = weights[:, None, :] * residual
            cross = summed[2] - jnp.dot(summed[3], alpha, precision=lax.Precision.HIGHEST)
            beta = -cholesky_solve(curvature, cross)
            search = scaled + combine(search, beta)
    return (solution, residual)


def solution(mesh):
    split = Mesh(
        mesh.devices.reshape(8, 12, 2, mesh.shape["dev"]), ("grp_0", "grp_1", "grp_2", "dev")
    )
    placed = (
        P(GRP_DEV, None, None),
        P(GRP_DEV, None, None),
        P(GRP_DEV, None),
        P(),
        P(GRP_DEV, None),
    )
    return jax.shard_map(
        body,
        mesh=split,
        in_specs=placed,
        out_specs=(P(GRP_DEV, None, None), P(GRP_DEV, None, None)),
        check_vma=False,
    )
```

profile of v0, /device:TPU:1, one launch (start us, length us, event | category | flops | bytes accessed | tf_op | source)
XLA Modules:
  0.0 284.3 jit_solution(7561023400426769355)
XLA Ops:
  10.7 5.8 %gather_fusion = bf16[1024,32]{1,0:T(8,128)(2,1)S(1)} fusion(bf16[2,32,512]{1,2,0:T(8,128)(2,1)S(1)} %copy.35, s32[1024]{0:T(1024)S(1)} %bitcast.218), kind=kCustom, calls=%fused_computation.clone | custom fusion | bytes 139264 | tf_op jit(solution)/shard_map/jit(take_along_axis)/gather | solution.py:81
  16.7 3.9 %collective-permute-start = (bf16[32,512]{1,0:T(8,128)(2,1)S(1)}, bf16[32,512]{1,0:T(8,128)(2,1)S(1)}, u32[]{:S(2)}, u32[]{:S(2)}) collective-permute-start(bf16[32,512]{1,0:T(8,128)(2,1)S(1)} %get-tuple-element.10), channel_id=1, source_target_pairs={{0,1},{1,2},{2,3},{3,4},{4,5},{5,6},{6,7},{7,8},{8,9},{9,10},{10,1... | collective-permute-start | bytes 98312 | tf_op jit(solution)/shard_map/ppermute | solution.py:33
  23.5 1.7 sort.19.cloned.1.call-done
  26.6 1.5 fusion.7
  28.1 1.5 convolution_bitcast_fusion.6
  29.6 1.5 convolution_bitcast_fusion.7
  31.1 3.7 %collective-permute-start.1 = (f32[32,512]{1,0:T(8,128)S(1)}, f32[32,512]{1,0:T(8,128)S(1)}, u32[]{:S(2)}, u32[]{:S(2)}) collective-permute-start(f32[32,512]{1,0:T(8,128)S(1)} %fusion.7), channel_id=1, source_target_pairs={{1,0},{2,1},{3,2},{4,3},{5,4},{6,5},{7,6},{8,7},{9,8},{10,9},{11,1... | collective-permute-start | bytes 196616 | tf_op jit(solution)/shard_map/ppermute | solution.py:33
  34.9 1.5 convolution_bitcast_fusion.8
  36.6 6.8 %gather_fusion.1 = f32[1024,32]{1,0:T(8,128)S(1)} fusion(f32[2,32,512]{1,2,0:T(8,128)S(1)} %copy.38, s32[1024]{0:T(1024)S(1)} %bitcast.220), kind=kCustom, calls=%fused_computation.1.clone | custom fusion | bytes 270336 | tf_op jit(solution)/shard_map/jit(take_along_axis)/gather | solution.py:96
  44.6 11.8 %all_to_all.10 = f32[4,1,4096]{2,1,0:T(1,128)S(1)} all-to-all(f32[4,1,4096]{2,1,0:T(1,128)S(1)} %reshape.160), channel_id=1, replica_groups=mesh['grp_0'=8,'grp_1'=12,'grp_2'=2,'dev'=4] {'dev'}, dimensions={0} | all-to-all | bytes 131072 | tf_op jit(solution)/shard_map/all_to_all | solution.py:16
  58.0 23.6 %psum.42 = f32[4,32,32]{1,2,0:T(8,128)S(1)} all-reduce(f32[4,32,32]{1,2,0:T(8,128)S(1)} %copy.41), channel_id=1, replica_groups=mesh['grp_0'=8,'grp_1'=12,'grp_2'=2,'dev'=4] {'grp_0'}, use_global_device_ids=true, to_apply=%region_2.4 | all-reduce | flops 4096 | bytes 32768 | tf_op jit(solution)/shard_map/psum | solution.py:27
  81.6 42.1 %psum.43 = f32[4,32,32]{1,2,0:T(8,128)S(1)} all-reduce(f32[4,32,32]{1,2,0:T(8,128)S(1)} %psum.42), channel_id=1, replica_groups=mesh['grp_0'=8,'grp_1'=12,'grp_2'=2,'dev'=4] {'grp_1'}, use_global_device_ids=true, to_apply=%region_3.5 | all-reduce | flops 4096 | bytes 32768 | tf_op jit(solution)/shard_map/psum | solution.py:27
  123.7 21.2 %psum.44 = f32[4,32,32]{1,2,0:T(8,128)S(1)} all-reduce(f32[4,32,32]{1,2,0:T(8,128)S(1)} %psum.43), channel_id=1, replica_groups=mesh['grp_0'=8,'grp_1'=12,'grp_2'=2,'dev'=4] {'grp_2'}, use_global_device_ids=true, to_apply=%region_4.6 | all-reduce | flops 4096 | bytes 32768 | tf_op jit(solution)/shard_map/psum | solution.py:27
  145.0 2.9 %cholesky.44 = f32[32,32]{1,0:T(8,128)S(1)} custom-call(f32[32,32]{1,0:T(8,128)S(1)} %fusion.34), custom_call_target="Cholesky" | custom-call | tf_op jit(solution)/shard_map/jit(cholesky)/cholesky | solution.py:37
  149.2 2.4 custom-call.23
  153.5 5.8 %gather_fusion.2 = bf16[1024,32]{1,0:T(8,128)(2,1)S(1)} fusion(bf16[2,32,512]{1,2,0:T(8,128)(2,1)S(1)} %copy.47, s32[1024]{0:T(1024)S(1)} %bitcast.219), kind=kCustom, calls=%fused_computation.2.clone | custom fusion | bytes 139264 | tf_op jit(solution)/shard_map/jit(take_along_axis)/gather | solution.py:81
  159.5 2.1 collective-permute-start.2
  161.8 4.1 %collective-permute-done.2 = bf16[32,512]{1,0:T(8,128)(2,1)S(1)} collective-permute-done((bf16[32,512]{1,0:T(8,128)(2,1)S(1)}, bf16[32,512]{1,0:T(8,128)(2,1)S(1)}, u32[]{:S(2)}, u32[]{:S(2)}) %collective-permute-start.2) | collective-permute-done | bytes 32800 | tf_op jit(solution)/shard_map/ppermute | solution.py:33
  165.9 1.5 fusion.5
  167.4 1.5 convolution_bitcast_fusion.3
  168.9 1.5 convolution_bitcast_fusion.4
  170.4 2.2 collective-permute-start.3
  172.7 1.5 convolution_bitcast_fusion.5
  174.2 1.3 collective-permute-done.3
  175.7 6.8 %gather_fusion.3 = f32[1024,32]{1,0:T(8,128)S(1)} fusion(f32[2,32,512]{1,2,0:T(8,128)S(1)} %copy.50, s32[1024]{0:T(1024)S(1)} %bitcast.221), kind=kCustom, calls=%fused_computation.3.clone | custom fusion | bytes 270336 | tf_op jit(solution)/shard_map/jit(take_along_axis)/gather | solution.py:96
  183.7 3.3 %all-to-all-start.1 = ((f32[4,1,2048]{2,1,0:T(1,128)}), f32[4,1,2048]{2,1,0:T(1,128)S(1)}, u32[]{:S(2)}, u32[]{:S(2)}) async-start(f32[4,1,2048]{2,1,0:T(1,128)} %reshape.162), calls=%async_computation.1 | async-start | bytes 65536 | tf_op jit(solution)/shard_map/all_to_all | solution.py:16
  187.3 3.9 %all-to-all-done.1 = f32[4,1,2048]{2,1,0:T(1,128)S(1)} async-done(((f32[4,1,2048]{2,1,0:T(1,128)}), f32[4,1,2048]{2,1,0:T(1,128)S(1)}, u32[]{:S(2)}, u32[]{:S(2)}) %all-to-all-start.1) | async-done | bytes 32800 | tf_op jit(solution)/shard_map/all_to_all | solution.py:16
  192.1 20.4 %psum.45 = f32[2,32,32]{1,2,0:T(8,128)S(1)} all-reduce(f32[2,32,32]{1,2,0:T(8,128)S(1)} %copy.53), channel_id=1, replica_groups=mesh['grp_0'=8,'grp_1'=12,'grp_2'=2,'dev'=4] {'grp_0'}, use_global_device_ids=true, to_apply=%region_8.0 | all-reduce | flops 2048 | bytes 16384 | tf_op jit(solution)/shard_map/psum | solution.py:27
  212.5 36.0 %psum.46 = f32[2,32,32]{1,2,0:T(8,128)S(1)} all-reduce(f32[2,32,32]{1,2,0:T(8,128)S(1)} %psum.45), channel_id=1, replica_groups=mesh['grp_0'=8,'grp_1'=12,'grp_2'=2,'dev'=4] {'grp_1'}, use_global_device_ids=true, to_apply=%region_9.0 | all-reduce | flops 2048 | bytes 16384 | tf_op jit(solution)/shard_map/psum | solution.py:27
  248.5 19.8 %psum.47 = f32[2,32,32]{1,2,0:T(8,128)S(1)} all-reduce(f32[2,32,32]{1,2,0:T(8,128)S(1)} %psum.46), channel_id=1, replica_groups=mesh['grp_0'=8,'grp_1'=12,'grp_2'=2,'dev'=4] {'grp_2'}, use_global_device_ids=true, to_apply=%region_10.15 | all-reduce | flops 2048 | bytes 16384 | tf_op jit(solution)/shard_map/psum | solution.py:27
  268.5 2.9 %cholesky.55 = f32[32,32]{1,0:T(8,128)S(1)} custom-call(f32[32,32]{1,0:T(8,128)S(1)} %fusion.33), custom_call_target="Cholesky" | custom-call | tf_op jit(solution)/shard_map/jit(cholesky)/cholesky | solution.py:37
  272.7 2.4 custom-call.29
  (83 shorter events, 20.6 us)
Async XLA Ops:
  7.2 18.0 %sort.19.cloned.1.call-start = ((), (), s32[]{:S(2)}) async-start(), calls=%async_computation.2 | async-start | bytes 24608 | tf_op jit(solution)/shard_map/jit(argsort)/sort | solution.py:76
  16.7 9.8 %collective-permute-start = (bf16[32,512]{1,0:T(8,128)(2,1)S(1)}, bf16[32,512]{1,0:T(8,128)(2,1)S(1)}, u32[]{:S(2)}, u32[]{:S(2)}) collective-permute-start(bf16[32,512]{1,0:T(8,128)(2,1)S(1)} %get-tuple-element.10), channel_id=1, source_target_pairs={{0,1},{1,2},{2,3},{3,4},{4,5},{5,6},{6,7},{7,8},{8,9},{9,10},{10,1... | collective-permute-start | bytes 98312 | tf_op jit(solution)/shard_map/ppermute | solution.py:33
  26.5 17.1 %copy-start = (f32[2,32,512]{2,1,0:T(8,128)S(1)}, f32[2,32,512]{2,1,0:T(8,128)}, u32[]{:S(2)}) copy-start(f32[2,32,512]{2,1,0:T(8,128)} %param.13) | copy-start | bytes 393220
  26.6 17.1 %copy-start.1 = (f32[2,512]{1,0:T(2,128)S(1)}, f32[2,512]{1,0:T(2,128)}, u32[]{:S(2)}) copy-start(f32[2,512]{1,0:T(2,128)} %param.14) | copy-start | bytes 12292
  31.1 5.2 %collective-permute-start.1 = (f32[32,512]{1,0:T(8,128)S(1)}, f32[32,512]{1,0:T(8,128)S(1)}, u32[]{:S(2)}, u32[]{:S(2)}) collective-permute-start(f32[32,512]{1,0:T(8,128)S(1)} %fusion.7), channel_id=1, source_target_pairs={{1,0},{2,1},{3,2},{4,3},{5,4},{6,5},{7,6},{8,7},{9,8},{10,9},{11,1... | collective-permute-start | bytes 196616 | tf_op jit(solution)/shard_map/ppermute | solution.py:33
  159.5 6.4 %collective-permute-start.2 = (bf16[32,512]{1,0:T(8,128)(2,1)S(1)}, bf16[32,512]{1,0:T(8,128)(2,1)S(1)}, u32[]{:S(2)}, u32[]{:S(2)}) collective-permute-start(bf16[32,512]{1,0:T(8,128)(2,1)S(1)} %get-tuple-element.8), channel_id=1, source_target_pairs={{0,1},{1,2},{2,3},{3,4},{4,5},{5,6},{6,7},{7,8},{8,9},{9,10},{10,1... | collective-permute-start | bytes 98312 | tf_op jit(solution)/shard_map/ppermute | solution.py:33
  170.4 5.0 %collective-permute-start.3 = (f32[32,512]{1,0:T(8,128)S(1)}, f32[32,512]{1,0:T(8,128)S(1)}, u32[]{:S(2)}, u32[]{:S(2)}) collective-permute-start(f32[32,512]{1,0:T(8,128)S(1)} %fusion.5), channel_id=1, source_target_pairs={{1,0},{2,1},{3,2},{4,3},{5,4},{6,5},{7,6},{8,7},{9,8},{10,9},{11,1... | collective-permute-start | bytes 196616 | tf_op jit(solution)/shard_map/ppermute | solution.py:33
  183.7 7.5 %all-to-all-start.1 = ((f32[4,1,2048]{2,1,0:T(1,128)}), f32[4,1,2048]{2,1,0:T(1,128)S(1)}, u32[]{:S(2)}, u32[]{:S(2)}) async-start(f32[4,1,2048]{2,1,0:T(1,128)} %reshape.162), calls=%async_computation.1 | async-start | bytes 65536 | tf_op jit(solution)/shard_map/all_to_all | solution.py:16
Sparse Core Ops, SparseCore 0:
  21.4 3.4 sort.21.cloned.1.call-done
  (1 shorter events, 0.0 us)
where the time goes:
time: 285 us; the launch traced here: 284 us
  blocking collectives  175 us (61%)
  local copies, waits for them, and re-layouts  31.7 us (11%)
  other arithmetic  19.9 us (7%)
  matrix products  18.6 us (7%)
  starting transfers between devices  15.3 us (5%)
  between operations  14.5 us (5%)
  waiting for transfers between devices  9.32 us (3%)
    psum x6, blocking collectives, over_axes(): return functools.reduce(lax.psum, axes, shard)  163 us
    gather x4, local copies, waits for them, and re-layouts, body(): gathered = jnp.take_along_axis(shifted, inverse[:, None, :], axis=2)  13.9 us
    dot_general x8, matrix products, column_part(): return jnp.dot(inputs, columns, preferred_element_type=jnp.float32)  12.1 us
    ppermute x4, starting transfers between devices, shifted_2(): return lax.ppermute(block, axis, route)  12 us
    gather x4, local copies, waits for them, and re-layouts, body(): turned = jnp.take_along_axis(search, slot_order[:, None, :], axis=2)  11.9 us
    all_to_all x1, blocking collectives, from_everyone(): lax.all_to_all(jnp.broadcast_to(shard[None], (peers, *shard.shape)), axis...  11.8 us
    another operation x6, other arithmetic, cholesky_solve(): factor = jnp.linalg.cholesky(matrix)  7.19 us
    another operation x4, other arithmetic, cholesky_solve(): lax.linalg.triangular_solve(factor, halfway, left_side=True, lower=True,...  6.17 us
  transfers between devices with their start and end apart: 5, of which 3 were waited for; matrix products, arithmetic and copies ran while one was open for 3% of the time, Pallas kernels for 0%

commit v1 on v0

v1 whole, which is shorter than its diff:
```python
import jax
import jax.numpy as jnp
from jax import lax
from jax.experimental import pallas as pl
from jax.experimental.pallas import tpu as pltpu
from jax.sharding import Mesh
from jax.sharding import PartitionSpec as P

GRP_DEV = ("grp_0", "grp_1", "grp_2", "dev")
F32 = jnp.float32
BF16 = jnp.bfloat16
HI = lax.Precision.HIGHEST
R = 32
B = 512
VM = pl.BlockSpec(memory_space=pltpu.VMEM)


def call(body, outs, n_in, smem=(), flops=10**8):
    return pl.pallas_call(
        body,
        out_shape=[jax.ShapeDtypeStruct(s, d) for s, d in outs],
        in_specs=[
            pl.BlockSpec(memory_space=pltpu.SMEM) if i in smem else VM for i in range(n_in)
        ],
        out_specs=[VM] * len(outs),
        compiler_params=pltpu.CompilerParams(vmem_limit_bytes=16 * 2**20),
        cost_estimate=pl.CostEstimate(flops=flops, bytes_accessed=2**20, transcendentals=0),
    )


def split(x):
    high = x.astype(BF16)
    return high, (x - high.astype(F32)).astype(BF16)


def pick(x, index):
    rows = x.shape[0]
    parts = []
    for out in range(B // 128):
        spread = jnp.broadcast_to(index[:, out * 128 : (out + 1) * 128], (rows, 128))
        low, high = spread & 127, spread >> 7
        part = None
        for source in range(B // 128):
            got = jnp.take_along_axis(
                x[:, source * 128 : (source + 1) * 128],
                low,
                axis=1,
                mode="promise_in_bounds",
            )
            part = got if part is None else jnp.where(high == source, got, part)
        parts.append(part)
    return jnp.concatenate(parts, axis=1)


def inverse_row(index):
    lane = lax.broadcasted_iota(jnp.int32, (128, 128), 1).astype(F32)
    place = lax.broadcasted_iota(jnp.int32, (128, 128), 0).astype(F32)
    values = index.astype(F32)
    sums = [None] * (B // 128)
    for source in range(B // 128):
        chunk = jnp.broadcast_to(values[:, source * 128 : (source + 1) * 128], (128, 128))
        column = chunk.T
        for out in range(B // 128):
            hit = jnp.where(column == lane + 128.0 * out, place + 128.0 * source, 0.0)
            sums[out] = hit if sums[out] is None else sums[out] + hit
    return jnp.concatenate([jnp.sum(s, axis=0, keepdims=True) for s in sums], axis=1)


def mm(x, y):
    return jnp.dot(x, y, preferred_element_type=F32)


def gram(x, y):
    return lax.dot_general(
        x, y, (((1,), (1,)), ((), ())), precision=HI, preferred_element_type=F32
    )


def begin(lens, forces, weights, order, r0, s0, rows, send):
    place = 0
    for axis in GRP_DEV:
        place = place * lax.axis_size(axis) + lax.axis_index(axis)
    lane = lax.broadcasted_iota(jnp.int32, (1, B), 1)
    for i in range(2):
        k = place * 2 + i
        live = jnp.where(k < lens.shape[0] - 1, lens[k], 0)
        mask = (lane < live).astype(F32)
        rows[i : i + 1, :] = mask
        rows[2 + i : 3 + i, :] = mask * weights[i : i + 1, :]
        field = mask * forces[i]
        r0[i] = field
        s0[i] = weights[i : i + 1, :] * field
    rows[4:8, :] = jnp.zeros((4, B), F32)
    stacked = jnp.concatenate([s0[1], jnp.broadcast_to(rows[3:4, :], (16, B))], axis=0)
    turned = pick(stacked, order[1:2, :])
    high, low = split(turned[:R])
    send[0:R, :] = high
    send[R : 2 * R, :] = low
    w = turned[R:]
    w1 = w.astype(BF16).astype(F32)
    w2 = (w - w1).astype(BF16).astype(F32)
    w3 = w - w1 - w2
    row = lax.broadcasted_iota(jnp.int32, (16, B), 0)
    send[2 * R : 2 * R + 16, :] = jnp.where(
        row == 0, w1, jnp.where(row == 1, w2, jnp.where(row == 2, w3, 0.0))
    ).astype(BF16)


def local_products(ops, s0, order, prod_b, part_a, forward, inv):
    inv[...] = jnp.concatenate(
        [inverse_row(order[0:1, :]), inverse_row(order[1:2, :]), jnp.zeros((6, B), F32)], axis=0
    ).astype(jnp.int32)
    t1, t2 = split(pick(s0[0], order[0:1, :]))
    b1, b2 = split(s0[1])
    x = jnp.concatenate(
        [jnp.concatenate([t1, b1], axis=1), jnp.concatenate([t2, b2], axis=1)], axis=0
    )
    prod = mm(x, ops[1])
    prod_b[...] = prod
    forward[...] = pick(prod[:R, B:], order[1:2, :])
    a1, a2 = split(s0[0])
    part_a[...] = mm(jnp.concatenate([a1, a2], axis=0), ops[0, B:, :])


def left_of_a(ops, came, part_a, back, left_low):
    left = part_a[:, :B] + mm(came[0 : 2 * R, :], ops[0, :B, :B])
    back[...] = left[:R]
    left_low[...] = left[R:]


def second_local(
    ops, came, came_right, part_a, back, left_low, prod_b, inv, rows, order, r0, s0,
    q_a, d_a, u_a, v_a, t_ua, part2_b, send_back, gpart,
):
    right = part_a[:, B:] + mm(came[0 : 2 * R, :], ops[0, :B, B:])
    both = right + pick(prod_b[:, :B], inv[0:1, :])
    q = rows[0:1, :] * both[:R]
    q_a[...] = q
    d_a[...] = rows[0:1, :] * both[R:]
    u = rows[2:3, :] * q
    u_a[...] = u
    w = came[2 * R : 2 * R + 16, :].astype(F32)
    w_prev = w[0:1] + w[1:2] + w[2:3]
    u_prev = w_prev * (came_right[...] + back[...])
    p1, p2 = split(u_prev)
    a1, a2 = split(u)
    x = jnp.concatenate(
        [jnp.concatenate([p1, a1], axis=1), jnp.concatenate([p2, a2], axis=1)], axis=0
    )
    prod = mm(x, ops[0])
    prod = prod[:R] + prod[R:]
    send_back[0:R, :] = prod[:, :B]
    send_back[R:, :] = left_low[...]
    v_a[...] = prod[:, B:]
    turned = pick(u, order[0:1, :])
    t_ua[...] = turned
    t1, t2 = split(turned)
    part = mm(jnp.concatenate([t1, t2], axis=0), ops[1, :B, :])
    part2_b[...] = part[:R] + part[R:]
    g4 = gram(jnp.concatenate([u_prev, u], axis=1), prod)
    g13 = gram(jnp.concatenate([s0[0], u], axis=0), q)
    g2 = gram(s0[0], r0[0]) + gram(s0[1], r0[1])
    gpart[...] = jnp.concatenate([g13[:R], g2, g13[R:], g4], axis=1)


def grams(ops, came_back, prod_b, inv, rows, s0, t_ua, part2_b, gpart, q_b, u_b, prod2_b, out):
    q = rows[1:2, :] * (prod_b[0:R, B:] + pick(came_back[...], inv[1:2, :]))
    q_b[...] = q
    u = rows[3:4, :] * q
    u_b[...] = u
    b1, b2 = split(u)
    prod = mm(jnp.concatenate([b1, b2], axis=0), ops[1, B:, :])
    prod = part2_b[...] + prod[:R] + prod[R:]
    prod2_b[...] = prod
    g4 = gram(jnp.concatenate([t_ua[...], u], axis=1), prod)
    g13 = gram(jnp.concatenate([s0[1], u], axis=0), q)
    out[...] = gpart[...] + jnp.concatenate(
        [g13[:R], jnp.zeros((R, R), F32), g13[R:], g4], axis=1
    )


def eliminate(m):
    row = lax.broadcasted_iota(jnp.int32, (R, 1), 0)
    for j in range(R):
        line = m[j : j + 1, :] / m[j : j + 1, j : j + 1]
        m = jnp.where(row == j, line, m - m[:, j : j + 1] * line)
    return m


def hdot(x, y):
    return jnp.dot(x, y, precision=HI, preferred_element_type=F32)


def finish(
    parts, came, prod_b, prod2_b, inv, rows, r0, s0, q_a, q_b, d_a, u_a, u_b, v_a, x_out, r_out
):
    g = parts[0]
    for i in range(1, parts.shape[0]):
        g = g + parts[i]
    gt = g.T
    g1, g2, g3, g4 = (g[:, i * R : (i + 1) * R] for i in range(4))
    g1t = gt[0:R, :]
    g4t = gt[3 * R : 4 * R, :]
    m = eliminate(jnp.concatenate([0.5 * (g1 + g1t), g2, g1t, g3], axis=1))
    alpha = m[:, R : 2 * R]
    eye = (
        lax.broadcasted_iota(jnp.int32, (R, R), 0) == lax.broadcasted_iota(jnp.int32, (R, R), 1)
    ).astype(F32)
    grown = eye - m[:, 2 * R : 3 * R] + hdot(m[:, 3 * R :], alpha)
    cross = g1t - hdot(g3, alpha)
    top = hdot(g1, grown) - hdot(g3, alpha)
    bottom = hdot(g3, grown) - hdot(0.5 * (g4 + g4t), alpha)
    flip = jnp.concatenate([grown, alpha, jnp.zeros((R, 2 * R), F32)], axis=1).T
    grown_t, alpha_t = flip[0:R, :], flip[R : 2 * R, :]
    curve = hdot(grown_t, top) - hdot(alpha_t, bottom)
    target = hdot(grown_t, g2 - hdot(g1, alpha)) - hdot(alpha_t, cross)
    curve_t = jnp.concatenate([curve, jnp.zeros((R, 3 * R), F32)], axis=1).T[0:R, :]
    m = eliminate(
        jnp.concatenate([0.5 * (curve + curve_t), target, jnp.zeros((R, 2 * R), F32)], axis=1)
    )
    alpha1 = m[:, R : 2 * R]
    onto_d = hdot(grown, alpha1)
    onto_u = hdot(alpha, alpha1)
    onto_s = alpha + onto_d
    coefficients = jnp.concatenate([onto_s, onto_d, onto_u, jnp.zeros((R, R), F32)], axis=1).T
    cs, cd, cu = coefficients[0:R], coefficients[R : 2 * R], coefficients[2 * R : 3 * R]
    d_right = rows[1:2, :] * (prod_b[R:, B:] + pick(came[R:, :], inv[1:2, :]))
    v_right = rows[1:2, :] * (prod2_b[:, B:] + pick(came[0:R, :], inv[1:2, :]))
    v_left = rows[0:1, :] * (v_a[...] + pick(prod2_b[:, :B], inv[0:1, :]))
    for i, q, d, u, v in ((0, q_a, d_a[...], u_a, v_left), (1, q_b, d_right, u_b, v_right)):
        x_out[i] = hdot(cs, s0[i]) - hdot(cu, u[...])
        r_out[i] = r0[i] - hdot(cs, q[...]) - hdot(cd, d) + hdot(cu, v)


def shifted(block, axes_size, distance):
    route = [(i, i + distance) for i in range(axes_size) if 0 <= i + distance < axes_size]
    return lax.ppermute(block, GRP_DEV, route)


def gathered(block, axes):
    spread = jnp.broadcast_to(block[None], (lax.axis_size(axes), *block.shape))
    return lax.all_to_all(spread, axes, 0, 0, tiled=True)


def body(operators, forces, weights, lengths, slot_order):
    devices = lax.axis_size(GRP_DEV)
    field, pair = ((R, B), F32), ((2, R, B), F32)
    r0, s0, rows, send = call(
        begin, [pair, pair, ((8, B), F32), ((2 * R + 16, B), BF16)], 4, smem=(0,)
    )(lengths, forces, weights, slot_order)
    came = shifted(send, devices, 1)
    prod_b, part_a, forward, inv = call(
        local_products,
        [((2 * R, 2 * B), F32), ((2 * R, 2 * B), F32), field, ((8, B), jnp.int32)],
        3,
    )(operators, s0, slot_order)
    came_right = shifted(forward, devices, 1)
    back, left_low = call(left_of_a, [field, field], 3)(operators, came, part_a)
    came_back = shifted(back, devices, -1)
    q_a, d_a, u_a, v_a, t_ua, part2_b, send_back, gpart = call(
        second_local,
        [field] * 5 + [((R, 2 * B), F32), ((2 * R, B), F32), ((R, 4 * R), F32)],
        12,
    )(
        operators, came, came_right, part_a, back, left_low, prod_b, inv, rows, slot_order, r0, s0
    )
    came_last = shifted(send_back, devices, -1)
    q_b, u_b, prod2_b, local = call(
        grams, [field, field, ((R, 2 * B), F32), ((R, 4 * R), F32)], 9
    )(operators, came_back, prod_b, inv, rows, s0, t_ua, part2_b, gpart)
    total = jnp.sum(gathered(local, ("grp_2", "dev")), axis=0)
    total = jnp.sum(gathered(total, "grp_0"), axis=0)
    parts = gathered(total, "grp_1")
    solution, residual = call(finish, [pair, pair], 14)(
        parts, came_last, prod_b, prod2_b, inv, rows, r0, s0, q_a, q_b, d_a, u_a, u_b, v_a
    )
    return (solution, residual)


def solution(mesh):
    split_mesh = Mesh(
        mesh.devices.reshape(8, 12, 2, mesh.shape["dev"]), ("grp_0", "grp_1", "grp_2", "dev")
    )
    return jax.shard_map(
        body,
        mesh=split_mesh,
        in_specs=(
            P(GRP_DEV, None, None),
            P(GRP_DEV, None, None),
            P(GRP_DEV, None),
            P(),
            P(GRP_DEV, None),
        ),
        out_specs=(P(GRP_DEV, None, None), P(GRP_DEV, None, None)),
        check_vma=False,
    )
```

time: 285 us -> 86.6 us (0.30)
  the two profiles are of different devices: /device:TPU:1 before, /device:TPU:2 now
where the time goes in v1:
time: 86.6 us; the launch traced here: 86.1 us
  blocking collectives  29.6 us (34%)
  starting transfers between devices  23.8 us (27%)
  waiting for transfers between devices  14 us (16%)
  Pallas kernels  12.1 us (14%)
  local copies, waits for them, and re-layouts  5.88 us (7%)
    all_to_all x2, blocking collectives, gathered(): return lax.all_to_all(spread, axes, 0, 0, tiled=True)  29.6 us
    ppermute x4, starting transfers between devices, shifted(): return lax.ppermute(block, GRP_DEV, route)  13.8 us
    all_to_all x1, starting transfers between devices, gathered(): return lax.all_to_all(spread, axes, 0, 0, tiled=True)  9.96 us
    pallas_call x1, Pallas kernels, body(): call(finish, [pair, pair], 14)  8.22 us
    ppermute x4, waiting for transfers between devices, shifted(): return lax.ppermute(block, GRP_DEV, route)  8.08 us
    all_to_all x1, waiting for transfers between devices, gathered(): return lax.all_to_all(spread, axes, 0, 0, tiled=True)  5.94 us
    unnamed x12, local copies, waits for them, and re-layouts  5.15 us
  transfers between devices with their start and end apart: 5, of which 5 were waited for; matrix products, arithmetic and copies ran while one was open for 0% of the time, Pallas kernels for 3%

profile of v1, /device:TPU:2, one launch (start us, length us, event | category | flops | bytes accessed | tf_op | source)
XLA Modules:
  0.0 86.1 jit_solution(16469217320728792455)
XLA Ops:
  0.6 0.0 copy-start.2
  0.6 0.7 copy-done.2
  1.3 0.0 copy-start.3
  1.3 0.9 %copy-done.3 = f32[2,32,512]{2,1,0:T(8,128)S(1)} copy-done((f32[2,32,512]{2,1,0:T(8,128)S(1)}, f32[2,32,512]{2,1,0:T(8,128)}, u32[]{:S(2)}) %copy-start.3) | copy-done | bytes 131096
  2.2 0.0 copy-start.4
  2.2 0.7 copy-done.4
  2.9 0.0 copy-start.5
  2.9 0.7 copy-done.5
  3.6 0.8 shard_map.68
  4.4 3.4 %collective-permute-start = (bf16[80,512]{1,0:T(8,128)(2,1)S(1)}, bf16[80,512]{1,0:T(8,128)(2,1)S(1)}, u32[]{:S(2)}, u32[]{:S(2)}) collective-permute-start(bf16[80,512]{1,0:T(8,128)(2,1)S(1)} %get-tuple-element.24), channel_id=1, source_target_pairs={{0,1},{1,2},{2,3},{3,4},{4,5},{5,6},{6,7},{7,8},{8,9},{9,10},{10,1... | collective-permute-start | bytes 245768 | tf_op jit(solution)/shard_map/ppermute | solution.py:237
  7.9 0.0 copy-start
  7.9 2.2 %copy-done = bf16[2,1024,1024]{2,1,0:T(8,128)(2,1)S(1)} copy-done((bf16[2,1024,1024]{2,1,0:T(8,128)(2,1)S(1)}, bf16[2,1024,1024]{2,1,0:T(8,128)(2,1)}, u32[]{:S(2)}) %copy-start) | copy-done | bytes 4194328
  10.0 0.0 copy-start.1
  10.0 1.0 %shard_map.69 = (f32[64,1024]{1,0:T(8,128)S(1)}, f32[64,1024]{1,0:T(8,128)S(1)}, f32[32,512]{1,0:T(8,128)S(1)}, s32[8,512]{1,0:T(8,128)S(1)}) custom-call(bf16[2,1024,1024]{2,1,0:T(8,128)(2,1)S(1)} %copy-done, f32[2,32,512]{2,1,0:T(8,128)S(1)} %get-tuple-element.25.s0, s32[2,512]{1,0:T(2,128)S(1)} %copy-done.2), custom_call_target="tpu_custom_call" | custom-call | flops 100000000 | bytes 1048576 | tf_op jit(solution)/shard_map/pallas_call | solution.py:252
  11.0 3.2 %collective-permute-start.2 = (f32[32,512]{1,0:T(8,128)S(1)}, f32[32,512]{1,0:T(8,128)S(1)}, u32[]{:S(2)}, u32[]{:S(2)}) collective-permute-start(f32[32,512]{1,0:T(8,128)S(1)} %get-tuple-element.31), channel_id=1, source_target_pairs={{0,1},{1,2},{2,3},{3,4},{4,5},{5,6},{6,7},{7,8},{8,9},{9,10},{10,1... | collective-permute-start | bytes 196616 | tf_op jit(solution)/shard_map/ppermute | solution.py:237
  14.3 3.4 %collective-permute-done.came = bf16[80,512]{1,0:T(8,128)(2,1)S(1)} collective-permute-done((bf16[80,512]{1,0:T(8,128)(2,1)S(1)}, bf16[80,512]{1,0:T(8,128)(2,1)S(1)}, u32[]{:S(2)}, u32[]{:S(2)}) %collective-permute-start) | collective-permute-done | bytes 81952 | tf_op jit(solution)/shard_map/ppermute | solution.py:237
  17.7 0.0 copy-done.1
  17.7 0.2 shard_map.70
  17.9 4.1 %collective-permute-start.1 = (f32[32,512]{1,0:T(8,128)S(1)}, f32[32,512]{1,0:T(8,128)S(1)}, u32[]{:S(2)}, u32[]{:S(2)}) collective-permute-start(f32[32,512]{1,0:T(8,128)S(1)} %get-tuple-element.27.back), channel_id=1, source_target_pairs={{1,0},{2,1},{3,2},{4,3},{5,4},{6,5},{7,6},{8,7},{9,8},{10,9},{11,1... | collective-permute-start | bytes 196616 | tf_op jit(solution)/shard_map/ppermute | solution.py:237
  22.0 0.1 collective-permute-done.2.came_right
  22.1 1.2 %shard_map.71 = (f32[32,512]{1,0:T(8,128)S(1)}, f32[32,512]{1,0:T(8,128)S(1)}, f32[32,512]{1,0:T(8,128)S(1)}, f32[32,512]{1,0:T(8,128)S(1)}, f32[32,512]{1,0:T(8...) custom-call(bf16[2,1024,1024]{2,1,0:T(8,128)(2,1)S(1)} %copy-done.1, ...), custom_call_target="tpu_custom_call" | custom-call | flops 100000000 | bytes 1048576 | tf_op jit(solution)/shard_map/pallas_call | solution.py:260
  23.2 0.8 collective-permute-done.1.came_back
  24.0 0.7 shard_map.72
  24.8 9.1 %all_to_all.15 = f32[8,32,128]{2,1,0:T(8,128)S(1)} all-to-all(f32[8,32,128]{2,1,0:T(8,128)S(1)} %broadcast_in_dim.6), channel_id=1, replica_groups=mesh['grp_0'=8,'grp_1'=12,'grp_2'=2,'dev'=4] {'grp_2','dev'}, dimensions={0} | all-to-all | bytes 262144 | tf_op jit(solution)/shard_map/all_to_all | solution.py:242
  33.9 20.5 %all_to_all.16 = f32[8,32,128]{2,1,0:T(8,128)S(1)} all-to-all(f32[8,32,128]{2,1,0:T(8,128)S(1)} %broadcast_in_dim.7), channel_id=1, replica_groups=mesh['grp_0'=8,'grp_1'=12,'grp_2'=2,'dev'=4] {'grp_0'}, dimensions={0} | all-to-all | bytes 262144 | tf_op jit(solution)/shard_map/all_to_all | solution.py:242
  54.4 0.7 broadcast_in_dim.8
  55.1 10.0 %all-to-all-start.2 = ((f32[12,32,128]{2,1,0:T(8,128)}), f32[12,32,128]{2,1,0:T(8,128)S(1)}, u32[]{:S(2)}, u32[]{:S(2)}) async-start(f32[12,32,128]{2,1,0:T(8,128)} %broadcast_in_dim.8), calls=%async_computation.2 | async-start | bytes 393216 | tf_op jit(solution)/shard_map/all_to_all | solution.py:242
  65.1 3.0 %collective-permute-start.3 = (f32[64,512]{1,0:T(8,128)S(1)}, f32[64,512]{1,0:T(8,128)S(1)}, u32[]{:S(2)}, u32[]{:S(2)}) collective-permute-start(f32[64,512]{1,0:T(8,128)S(1)} %get-tuple-element.38), channel_id=1, source_target_pairs={{1,0},{2,1},{3,2},{4,3},{5,4},{6,5},{7,6},{8,7},{9,8},{10,9},{11,1... | collective-permute-start | bytes 393224 | tf_op jit(solution)/shard_map/ppermute | solution.py:237
  68.1 3.8 %collective-permute-done.3.came = f32[64,512]{1,0:T(8,128)S(1)} collective-permute-done((f32[64,512]{1,0:T(8,128)S(1)}, f32[64,512]{1,0:T(8,128)S(1)}, u32[]{:S(2)}, u32[]{:S(2)}) %collective-permute-start.3) | collective-permute-done | bytes 131104 | tf_op jit(solution)/shard_map/ppermute | solution.py:237
  71.9 5.9 %all-to-all-done.2.parts = f32[12,32,128]{2,1,0:T(8,128)S(1)} async-done(((f32[12,32,128]{2,1,0:T(8,128)}), f32[12,32,128]{2,1,0:T(8,128)S(1)}, u32[]{:S(2)}, u32[]{:S(2)}) %all-to-all-start.2) | async-done | bytes 196640 | tf_op jit(solution)/shard_map/all_to_all | solution.py:242
  77.9 8.2 %shard_map.73 = (f32[2,32,512]{2,1,0:T(8,128)}, f32[2,32,512]{2,1,0:T(8,128)}) custom-call(f32[12,32,128]{2,1,0:T(8,128)S(1)} %all-to-all-done.2.parts, f32[64,512]{1,0:T(8,128)S(1)} %collective-permute-done.3.came, f32[64,1024]{1,0:T(8,128)S(1)} %get-tuple-element.28.prod_b, f32[32,1024]{1,0:T(8,128)S(1)} %get-tuple-element.39.prod2_b, ...), custom_call_target="tpu_custom_call" | custom-call | flops 100000000 | bytes 1048576 | tf_op jit(solution)/shard_map/pallas_call | solution.py:274
  (4 shorter events, 0.1 us)
Async XLA Ops:
  0.6 0.7 copy-start.2
  1.3 0.9 %copy-start.3 = (f32[2,32,512]{2,1,0:T(8,128)S(1)}, f32[2,32,512]{2,1,0:T(8,128)}, u32[]{:S(2)}) copy-start(f32[2,32,512]{2,1,0:T(8,128)} %forces.1) | copy-start | bytes 393220
  2.2 0.7 copy-start.4
  2.9 0.7 copy-start.5
  4.4 13.2 %collective-permute-start = (bf16[80,512]{1,0:T(8,128)(2,1)S(1)}, bf16[80,512]{1,0:T(8,128)(2,1)S(1)}, u32[]{:S(2)}, u32[]{:S(2)}) collective-permute-start(bf16[80,512]{1,0:T(8,128)(2,1)S(1)} %get-tuple-element.24), channel_id=1, source_target_pairs={{0,1},{1,2},{2,3},{3,4},{4,5},{5,6},{6,7},{7,8},{8,9},{9,10},{10,1... | collective-permute-start | bytes 245768 | tf_op jit(solution)/shard_map/ppermute | solution.py:237
  7.9 2.2 %copy-start = (bf16[2,1024,1024]{2,1,0:T(8,128)(2,1)S(1)}, bf16[2,1024,1024]{2,1,0:T(8,128)(2,1)}, u32[]{:S(2)}) copy-start(bf16[2,1024,1024]{2,1,0:T(8,128)(2,1)} %ops.7) | copy-start | bytes 12582916
  10.0 7.6 %copy-start.1 = (bf16[2,1024,1024]{2,1,0:T(8,128)(2,1)S(1)}, bf16[2,1024,1024]{2,1,0:T(8,128)(2,1)}, u32[]{:S(2)}) copy-start(bf16[2,1024,1024]{2,1,0:T(8,128)(2,1)} %ops.7) | copy-start | bytes 12582916
  11.0 11.1 %collective-permute-start.2 = (f32[32,512]{1,0:T(8,128)S(1)}, f32[32,512]{1,0:T(8,128)S(1)}, u32[]{:S(2)}, u32[]{:S(2)}) collective-permute-start(f32[32,512]{1,0:T(8,128)S(1)} %get-tuple-element.31), channel_id=1, source_target_pairs={{0,1},{1,2},{2,3},{3,4},{4,5},{5,6},{6,7},{7,8},{8,9},{9,10},{10,1... | collective-permute-start | bytes 196616 | tf_op jit(solution)/shard_map/ppermute | solution.py:237
  17.9 6.2 %collective-permute-start.1 = (f32[32,512]{1,0:T(8,128)S(1)}, f32[32,512]{1,0:T(8,128)S(1)}, u32[]{:S(2)}, u32[]{:S(2)}) collective-permute-start(f32[32,512]{1,0:T(8,128)S(1)} %get-tuple-element.27.back), channel_id=1, source_target_pairs={{1,0},{2,1},{3,2},{4,3},{5,4},{6,5},{7,6},{8,7},{9,8},{10,9},{11,1... | collective-permute-start | bytes 196616 | tf_op jit(solution)/shard_map/ppermute | solution.py:237
  55.1 22.8 %all-to-all-start.2 = ((f32[12,32,128]{2,1,0:T(8,128)}), f32[12,32,128]{2,1,0:T(8,128)S(1)}, u32[]{:S(2)}, u32[]{:S(2)}) async-start(f32[12,32,128]{2,1,0:T(8,128)} %broadcast_in_dim.8), calls=%async_computation.2 | async-start | bytes 393216 | tf_op jit(solution)/shard_map/all_to_all | solution.py:242
  65.1 6.9 %collective-permute-start.3 = (f32[64,512]{1,0:T(8,128)S(1)}, f32[64,512]{1,0:T(8,128)S(1)}, u32[]{:S(2)}, u32[]{:S(2)}) collective-permute-start(f32[64,512]{1,0:T(8,128)S(1)} %get-tuple-element.38), channel_id=1, source_target_pairs={{1,0},{2,1},{3,2},{4,3},{5,4},{6,5},{7,6},{8,7},{9,8},{10,9},{11,1... | collective-permute-start | bytes 393224 | tf_op jit(solution)/shard_map/ppermute | solution.py:237
